TPU v7x, 512 devices: a whole 4x4x16 slice. The times are simulated.
512 devices in a mesh: quad: 16 (over z_lo, core), gy: 8 (over y, z_hi), gx: 4 (over x).
Axes of the slice: x: 4, y: 4, z: 16 (z_hi: 2, z_lo: 8; z = z_hi * 8 + z_lo), core: 2. Of those that a mesh axis runs over, the one named last changes fastest.
Arguments:
- modes_now: bfloat16 [1024, 64, 512], P('quad', 'gy', 'gx'), may hold values from -4 to 4
- basis_rows: bfloat16 [4096, 1024], P('quad'), may hold values from -0.25 to 0.25
- quad_weights: float32 [4096], P('quad'), may hold values from 0.2 to 2
- germ_nodes: float32 [4096, 8], P('quad'), may hold values from -1.5 to 1.5
- log_fields: float32 [8, 64, 512], P(None, 'gy', 'gx'), may hold values from -1 to 1
- reaction_rates: float32 [4096], P('quad'), may hold values from 0.08 to 0.32
Outputs:
- modes_next: float32 [1024, 64, 512], P('quad', 'gy', 'gx')
All inputs are finite; a program needn't handle non-finite values.
Results may differ from a plain program's by a relative error of at most 0.02.
Values may be sent and summed in bfloat16 or wider, within the bound.
No kernel may reach another device: no remote copies, remote signals or barrier semaphores. Data moves between devices by JAX's collectives and lax.ppermute only.
A program may use at most 64 MiB of HBM per device.

v0:
```python
import jax
import jax.numpy as jnp
from jax import lax
from jax.sharding import PartitionSpec as P

time_step = 0.04


def with_halo(array, sides, width):
    for axis, dim in sides:
        peers, length = (lax.axis_size(axis), array.shape[dim])
        up = [(i, (i + 1) % peers) for i in range(peers - 1)]
        down = [(j, i) for i, j in up]
        last = lax.slice_in_dim(array, length - width, length, axis=dim)
        leading = lax.slice_in_dim(array, 0, width, axis=dim)
        before = lax.ppermute(last, axis, up)
        after = lax.ppermute(leading, axis, down)
        array = jnp.concatenate([before, array, after], axis=dim)
    return array


def neighbour(array, drow, dcol):
    return array[:, 1 + drow : array.shape[1] - 1 + drow, 1 + dcol : array.shape[2] - 1 + dcol]


def drive_with(field_ext, coeff_ext, rates, weights):
    center = neighbour(field_ext, 0, 0)
    coeff_mid = neighbour(coeff_ext, 0, 0)
    total = jnp.zeros_like(center)
    for drow, dcol in ((-1, 0), (1, 0), (0, -1), (0, 1)):
        total = total + (coeff_mid + neighbour(coeff_ext, drow, dcol)) * (
            neighbour(field_ext, drow, dcol) - center
        )
    total = total + rates[:, None, None] * (center - center * center * center)
    return (weights[:, None, None] * total).astype(jnp.bfloat16).reshape(center.shape[0], -1)


def rim_fields(field):
    return with_halo(field, (("gy", 1), ("gx", 2)), 1)


def body(modes_now, basis_rows, quad_weights, germ_nodes, log_fields, reaction_rates):
    k_local, rows_y, cols_x = modes_now.shape
    q_local, modes_total = basis_rows.shape
    log_ext = with_halo(log_fields, (("gy", 1), ("gx", 2)), 1)
    coeff_ext = jnp.exp(
        jnp.einsum("qj,jyx->qyx", germ_nodes, log_ext, precision=lax.Precision.HIGHEST)
    )

    def realize(block_flat):
        return jnp.dot(
            basis_rows,
            lax.all_gather(block_flat, "quad", axis=0, tiled=True),
            preferred_element_type=jnp.float32,
        )

    def field_of(block):
        return rim_fields(realize(block.reshape(k_local, -1)).reshape(q_local, rows_y, cols_x))

    def drive(field_ext):
        return drive_with(field_ext, coeff_ext, reaction_rates, quad_weights)

    def spread(weighted):
        return (
            lax.psum_scatter(
                lax.dot_general(
                    basis_rows,
                    weighted,
                    (((0,), (0,)), ((), ())),
                    preferred_element_type=jnp.float32,
                ).astype(jnp.bfloat16),
                "quad",
                scatter_dimension=0,
                tiled=True,
            )
            .astype(jnp.float32)
            .reshape(k_local, rows_y, cols_x)
        )

    current = modes_now.astype(jnp.float32)
    first = spread(drive(field_of(modes_now)))
    iterate_one = (current + time_step * first).astype(jnp.bfloat16)
    field_one = field_of(iterate_one)
    second = spread(drive(field_one))
    return current + time_step * second


def solution(mesh):
    in_specs = (
        P("quad", "gy", "gx"),
        P("quad", None),
        P("quad"),
        P("quad", None),
        P(None, "gy", "gx"),
        P("quad"),
    )
    out_specs = P("quad", "gy", "gx")
    return jax.shard_map(body, mesh=mesh, in_specs=in_specs, out_specs=out_specs, check_vma=False)
```

profile of v0, /device:TPU:4, one launch (start us, length us, event | category | flops | bytes accessed | tf_op | source)
XLA Modules:
  0.0 528.8 jit_solution(11073676379611655207)
XLA Ops:
  6.5 1.6 copy.32
  9.1 15.7 %collective-permute-start = (f32[8,1,128]{2,0,1:T(8,128)S(1)}, f32[8,1,128]{2,0,1:T(8,128)S(1)}, u32[]{:S(2)}, u32[]{:S(2)}) collective-permute-start(f32[8,1,128]{2,0,1:T(8,128)S(1)} %copy.29), channel_id=1, source_target_pairs={{0,4},{4,8},{8,12},{12,16},{16,20},{20,24},{24,28},{1,5},{5,9},{9,... | collective-permute-start | bytes 12296 | tf_op jit(solution)/shard_map/ppermute | solution.py:16
  24.8 1.3 collective-permute-start.1
  26.9 12.2 %collective-permute-done.1 = f32[8,1,128]{2,0,1:T(8,128)S(1)} collective-permute-done((f32[8,1,128]{2,0,1:T(8,128)S(1)}, f32[8,1,128]{2,0,1:T(8,128)S(1)}, u32[]{:S(2)}, u32[]{:S(2)}) %collective-permute-start.1) | collective-permute-done | bytes 4128 | tf_op jit(solution)/shard_map/ppermute | solution.py:17
  39.2 75.3 %all-gather.3.cloned.1.call-done = bf16[1024,1024]{1,0:T(8,128)(2,1)} async-done(((bf16[64,1024]{1,0:T(8,128)(2,1)}), bf16[1024,1024]{1,0:T(8,128)(2,1)}) %all-gather.3.cloned.1.call-update) | async-done | bytes 2097168 | tf_op jit(solution)/shard_map/all_gather | solution.py:53
  114.5 2.5 fusion.43
  117.1 16.9 %collective-permute-start.4 = (f32[256,1,128]{0,2,1:T(8,128)S(1)}, f32[256,1,128]{0,2,1:T(8,128)S(1)}, u32[]{:S(2)}, u32[]{:S(2)}) collective-permute-start(f32[256,1,128]{0,2,1:T(8,128)S(1)} %get-tuple-element.11), channel_id=1, source_target_pairs={{0,4},{4,8},{8,12},{12,16},{16,20},{20,24},{24,28},{1,5},{5,9},{9,... | collective-permute-start | bytes 393224 | tf_op jit(solution)/shard_map/ppermute | solution.py:16
  133.9 1.3 collective-permute-start.5
  135.3 3.1 collective-permute-start.2
  138.4 2.7 collective-permute-start.3
  141.2 8.3 %collective-permute-done.5 = f32[256,1,128]{0,2,1:T(8,128)S(1)} collective-permute-done((f32[256,1,128]{0,2,1:T(8,128)S(1)}, f32[256,1,128]{0,2,1:T(8,128)S(1)}, u32[]{:S(2)}, u32[]{:S(2)}) %collective-permute-start.5) | collective-permute-done | bytes 131104 | tf_op jit(solution)/shard_map/ppermute | solution.py:17
  149.5 3.1 collective-permute-start.6
  152.7 2.7 collective-permute-start.7
  155.4 1.5 fusion
  157.0 1.3 collective-permute-done.7
  158.2 1.3 fusion.4
  159.6 2.0 convert_bitcast_fusion.1
  161.6 3.9 copy.20
  165.6 105.7 %reduce-scatter.7.cloned.1.call-done = bf16[64,1024]{1,0:T(8,128)(2,1)} async-done(((bf16[1024,1024]{1,0:T(8,128)(2,1)}), bf16[64,1024]{1,0:T(8,128)(2,1)}) %reduce-scatter.7.cloned.1.call-update) | async-done | bytes 131088
  271.3 1.1 copy.21
  273.4 94.9 %all-gather.5.cloned.1.call-done = bf16[1024,1024]{1,0:T(8,128)(2,1)} async-done(((bf16[64,1024]{1,0:T(8,128)(2,1)}), bf16[1024,1024]{1,0:T(8,128)(2,1)}) %all-gather.5.cloned.1.call-update) | async-done | bytes 2097168 | tf_op jit(solution)/shard_map/all_gather | solution.py:53
  368.3 2.4 fusion.44
  370.7 17.0 %collective-permute-start.8 = (f32[256,1,128]{0,2,1:T(8,128)S(1)}, f32[256,1,128]{0,2,1:T(8,128)S(1)}, u32[]{:S(2)}, u32[]{:S(2)}) collective-permute-start(f32[256,1,128]{0,2,1:T(8,128)S(1)} %get-tuple-element.9), channel_id=1, source_target_pairs={{0,4},{4,8},{8,12},{12,16},{16,20},{20,24},{24,28},{1,5},{5,9},{9,... | collective-permute-start | bytes 393224 | tf_op jit(solution)/shard_map/ppermute | solution.py:16
  387.7 1.3 collective-permute-start.9
  389.0 1.2 collective-permute-done.8
  390.1 13.1 %collective-permute-done.9 = f32[256,1,128]{0,2,1:T(8,128)S(1)} collective-permute-done((f32[256,1,128]{0,2,1:T(8,128)S(1)}, f32[256,1,128]{0,2,1:T(8,128)S(1)}, u32[]{:S(2)}, u32[]{:S(2)}) %collective-permute-start.9) | collective-permute-done | bytes 131104 | tf_op jit(solution)/shard_map/ppermute | solution.py:17
  403.2 1.9 collective-permute-start.10
  405.2 3.9 collective-permute-start.11
  409.1 1.6 collective-permute-done.11
  410.7 1.3 fusion.8
  412.8 2.6 copy.22
  415.4 104.8 %reduce-scatter.9.cloned.1.call-done = bf16[64,1024]{1,0:T(8,128)(2,1)} async-done(((bf16[1024,1024]{1,0:T(8,128)(2,1)}), bf16[64,1024]{1,0:T(8,128)(2,1)}) %reduce-scatter.9.cloned.1.call-update) | async-done | bytes 131088
  (44 shorter events, 5.7 us)
Async XLA Ops:
  6.5 107.9 %copy-start = (bf16[256,1024]{1,0:T(8,128)(2,1)S(1)}, bf16[256,1024]{1,0:T(8,128)(2,1)}, u32[]{:S(2)}) copy-start(bf16[256,1024]{1,0:T(8,128)(2,1)} %param.7) | copy-start | bytes 1572868
  6.5 107.9 %all-gather.3.cloned.1.call-start = ((), (), s32[]{:S(2)}) async-start(), calls=%async_computation.2 | async-start | bytes 2228224 | tf_op jit(solution)/shard_map/all_gather | solution.py:53
  8.2 263.1 %reduce-scatter.7.cloned.1.call-start = ((), (), s32[]{:S(2)}) async-start(), calls=%async_computation.4 | async-start | bytes 2228224
  9.1 17.0 %collective-permute-start = (f32[8,1,128]{2,0,1:T(8,128)S(1)}, f32[8,1,128]{2,0,1:T(8,128)S(1)}, u32[]{:S(2)}, u32[]{:S(2)}) collective-permute-start(f32[8,1,128]{2,0,1:T(8,128)S(1)} %copy.29), channel_id=1, source_target_pairs={{0,4},{4,8},{8,12},{12,16},{16,20},{20,24},{24,28},{1,5},{5,9},{9,... | collective-permute-start | bytes 12296 | tf_op jit(solution)/shard_map/ppermute | solution.py:16
  24.8 14.3 %collective-permute-start.1 = (f32[8,1,128]{2,0,1:T(8,128)S(1)}, f32[8,1,128]{2,0,1:T(8,128)S(1)}, u32[]{:S(2)}, u32[]{:S(2)}) collective-permute-start(f32[8,1,128]{2,0,1:T(8,128)S(1)} %copy.30), channel_id=1, source_target_pairs={{4,0},{8,4},{12,8},{16,12},{20,16},{24,20},{28,24},{5,1},{9,5},{13... | collective-permute-start | bytes 12296 | tf_op jit(solution)/shard_map/ppermute | solution.py:17
  39.2 116.3 %copy-start.2 = (f32[256,8]{0,1:T(8,128)S(1)}, f32[256,8]{0,1:T(8,128)}, u32[]{:S(2)}) copy-start(f32[256,8]{0,1:T(8,128)} %param.9) | copy-start | bytes 24580
  117.0 41.2 %copy-start.3 = (f32[256]{0:T(256)S(1)}, f32[256]{0:T(256)}, u32[]{:S(2)}) copy-start(f32[256]{0:T(256)} %param.11) | copy-start | bytes 3076
  117.0 41.2 %copy-start.4 = (f32[256]{0:T(256)S(1)}, f32[256]{0:T(256)}, u32[]{:S(2)}) copy-start(f32[256]{0:T(256)} %param.8) | copy-start | bytes 3076
  117.1 24.1 %collective-permute-start.4 = (f32[256,1,128]{0,2,1:T(8,128)S(1)}, f32[256,1,128]{0,2,1:T(8,128)S(1)}, u32[]{:S(2)}, u32[]{:S(2)}) collective-permute-start(f32[256,1,128]{0,2,1:T(8,128)S(1)} %get-tuple-element.11), channel_id=1, source_target_pairs={{0,4},{4,8},{8,12},{12,16},{16,20},{20,24},{24,28},{1,5},{5,9},{9,... | collective-permute-start | bytes 393224 | tf_op jit(solution)/shard_map/ppermute | solution.py:16
  133.9 15.6 %collective-permute-start.5 = (f32[256,1,128]{0,2,1:T(8,128)S(1)}, f32[256,1,128]{0,2,1:T(8,128)S(1)}, u32[]{:S(2)}, u32[]{:S(2)}) collective-permute-start(f32[256,1,128]{0,2,1:T(8,128)S(1)} %get-tuple-element.12), channel_id=1, source_target_pairs={{4,0},{8,4},{12,8},{16,12},{20,16},{24,20},{28,24},{5,1},{9,5},{13... | collective-permute-start | bytes 393224 | tf_op jit(solution)/shard_map/ppermute | solution.py:17
  135.3 20.1 %collective-permute-start.2 = (f32[8,10,1]{2,0,1:T(8,128)S(1)}, f32[8,10,1]{2,0,1:T(8,128)S(1)}, u32[]{:S(2)}, u32[]{:S(2)}) collective-permute-start(f32[8,10,1]{2,0,1:T(8,128)S(1)} %get-tuple-element.13), channel_id=1, source_target_pairs={{0,1},{1,2},{2,3},{4,5},{5,6},{6,7},{8,9},{9,10},{10,11},{12,13},{... | collective-permute-start | bytes 968 | tf_op jit(solution)/shard_map/ppermute | solution.py:16
  138.4 17.0 %collective-permute-start.3 = (f32[8,10,1]{2,0,1:T(8,128)S(1)}, f32[8,10,1]{2,0,1:T(8,128)S(1)}, u32[]{:S(2)}, u32[]{:S(2)}) collective-permute-start(f32[8,10,1]{2,0,1:T(8,128)S(1)} %get-tuple-element.14), channel_id=1, source_target_pairs={{1,0},{2,1},{3,2},{5,4},{6,5},{7,6},{9,8},{10,9},{11,10},{13,12},{... | collective-permute-start | bytes 968 | tf_op jit(solution)/shard_map/ppermute | solution.py:17
  149.5 7.4 %collective-permute-start.6 = (f32[256,10,1]{0,2,1:T(1,128)S(1)}, f32[256,10,1]{0,2,1:T(1,128)S(1)}, u32[]{:S(2)}, u32[]{:S(2)}) collective-permute-start(f32[256,10,1]{0,2,1:T(1,128)S(1)} %get-tuple-element.7), channel_id=1, source_target_pairs={{0,1},{1,2},{2,3},{4,5},{5,6},{6,7},{8,9},{9,10},{10,11},{12,13},{... | collective-permute-start | bytes 30728 | tf_op jit(solution)/shard_map/ppermute | solution.py:16
  152.7 5.6 %collective-permute-start.7 = (f32[256,10,1]{0,2,1:T(1,128)S(1)}, f32[256,10,1]{0,2,1:T(1,128)S(1)}, u32[]{:S(2)}, u32[]{:S(2)}) collective-permute-start(f32[256,10,1]{0,2,1:T(1,128)S(1)} %get-tuple-element.8), channel_id=1, source_target_pairs={{1,0},{2,1},{3,2},{5,4},{6,5},{7,6},{9,8},{10,9},{11,10},{13,12},{... | collective-permute-start | bytes 30728 | tf_op jit(solution)/shard_map/ppermute | solution.py:17
  165.5 107.1 %copy-start.1 = (bf16[64,8,128]{2,1,0:T(8,128)(2,1)S(1)}, bf16[64,8,128]{2,1,0:T(8,128)(2,1)}, u32[]{:S(2)}) copy-start(bf16[64,8,128]{2,1,0:T(8,128)(2,1)} %param.6) | copy-start | bytes 393220
  165.6 202.7 %all-gather.5.cloned.1.call-start = ((), (), s32[]{:S(2)}) async-start(), calls=%async_computation.3 | async-start | bytes 2228224 | tf_op jit(solution)/shard_map/all_gather | solution.py:53
  273.4 246.9 %reduce-scatter.9.cloned.1.call-start = ((), (), s32[]{:S(2)}) async-start(), calls=%async_computation.5 | async-start | bytes 2228224
  370.7 19.5 %collective-permute-start.8 = (f32[256,1,128]{0,2,1:T(8,128)S(1)}, f32[256,1,128]{0,2,1:T(8,128)S(1)}, u32[]{:S(2)}, u32[]{:S(2)}) collective-permute-start(f32[256,1,128]{0,2,1:T(8,128)S(1)} %get-tuple-element.9), channel_id=1, source_target_pairs={{0,4},{4,8},{8,12},{12,16},{16,20},{20,24},{24,28},{1,5},{5,9},{9,... | collective-permute-start | bytes 393224 | tf_op jit(solution)/shard_map/ppermute | solution.py:16
  387.7 15.6 %collective-permute-start.9 = (f32[256,1,128]{0,2,1:T(8,128)S(1)}, f32[256,1,128]{0,2,1:T(8,128)S(1)}, u32[]{:S(2)}, u32[]{:S(2)}) collective-permute-start(f32[256,1,128]{0,2,1:T(8,128)S(1)} %get-tuple-element.10), channel_id=1, source_target_pairs={{4,0},{8,4},{12,8},{16,12},{20,16},{24,20},{28,24},{5,1},{9,5},{13... | collective-permute-start | bytes 393224 | tf_op jit(solution)/shard_map/ppermute | solution.py:17
  403.2 5.9 %collective-permute-start.10 = (f32[256,10,1]{0,2,1:T(1,128)S(1)}, f32[256,10,1]{0,2,1:T(1,128)S(1)}, u32[]{:S(2)}, u32[]{:S(2)}) collective-permute-start(f32[256,10,1]{0,2,1:T(1,128)S(1)} %get-tuple-element.5), channel_id=1, source_target_pairs={{0,1},{1,2},{2,3},{4,5},{5,6},{6,7},{8,9},{9,10},{10,11},{12,13},{... | collective-permute-start | bytes 30728 | tf_op jit(solution)/shard_map/ppermute | solution.py:16
  405.2 5.6 %collective-permute-start.11 = (f32[256,10,1]{0,2,1:T(1,128)S(1)}, f32[256,10,1]{0,2,1:T(1,128)S(1)}, u32[]{:S(2)}, u32[]{:S(2)}) collective-permute-start(f32[256,10,1]{0,2,1:T(1,128)S(1)} %get-tuple-element.6), channel_id=1, source_target_pairs={{1,0},{2,1},{3,2},{5,4},{6,5},{7,6},{9,8},{10,9},{11,10},{13,12},{... | collective-permute-start | bytes 30728 | tf_op jit(solution)/shard_map/ppermute | solution.py:17
Sparse Core Ops, SparseCore 0:
  9.4 105.0 all-gather.2
  165.7 105.5 reduce-scatter.6
  273.5 94.7 all-gather.4
  415.5 104.6 reduce-scatter.8
where the time goes:
time: 530 us; the launch traced here: 529 us
  waiting for transfers between devices  418 us (79%)
  starting transfers between devices  71.1 us (13%)
  between operations  13.4 us (3%)
  local copies, waits for them, and re-layouts  13.1 us (2%)
  matrix products  9.15 us (2%)
    unnamed x6, waiting for transfers between devices  211 us
    all_gather x2, waiting for transfers between devices, realize(): lax.all_gather(block_flat, 'quad', axis=0, tiled=True)  170 us
    ppermute x6, starting transfers between devices, with_halo(): before = lax.ppermute(last, axis, up)  57.7 us
    ppermute x6, waiting for transfers between devices, with_halo(): after = lax.ppermute(leading, axis, down)  36.5 us
    ppermute x6, starting transfers between devices, with_halo(): after = lax.ppermute(leading, axis, down)  13.2 us
    unnamed x20, local copies, waits for them, and re-layouts  11.8 us
  transfers between devices with their start and end apart: 16, of which 10 were waited for; matrix products, arithmetic and copies ran while one was open for 1% of the time, Pallas kernels for 0%

commit v1 on v0

--- a/solution.py
+++ b/solution.py
@@ -50,7 +50,10 @@
     def realize(block_flat):
         return jnp.dot(
             basis_rows,
-            lax.all_gather(block_flat, "quad", axis=0, tiled=True),
+            jnp.concatenate(
+                lax.all_to_all(jnp.stack([block_flat] * lax.axis_size("quad")), "quad", 0, 0),
+                axis=0,
+            ),
             preferred_element_type=jnp.float32,
         )
 

time: 530 us -> 547 us (1.032)
  the two profiles are of different devices: /device:TPU:4 before, /device:TPU:2 now
where the time goes in v1:
time: 547 us; the launch traced here: 546 us
  waiting for transfers between devices  348 us (64%)
  blocking collectives  96.9 us (18%)
  starting transfers between devices  62.4 us (11%)
  local copies, waits for them, and re-layouts  16.2 us (3%)
  between operations  13.8 us (3%)
  matrix products  5.78 us (1%)
    unnamed x4, waiting for transfers between devices  247 us
    all_to_all x1, blocking collectives, realize(): lax.all_to_all(jnp.stack([block_flat] * lax.axis_size('quad')), 'quad', 0...  96.9 us
    ppermute x6, starting transfers between devices, with_halo(): before = lax.ppermute(last, axis, up)  38.3 us
    ppermute x6, waiting for transfers between devices, with_halo(): before = lax.ppermute(last, axis, up)  36 us
    all_to_all x1, waiting for transfers between devices, realize(): lax.all_to_all(jnp.stack([block_flat] * lax.axis_size('quad')), 'quad', 0...  33 us
    ppermute x6, waiting for transfers between devices, with_halo(): after = lax.ppermute(leading, axis, down)  32.4 us
    all_to_all x1, starting transfers between devices, realize(): lax.all_to_all(jnp.stack([block_flat] * lax.axis_size('quad')), 'quad', 0...  12.8 us
    ppermute x6, starting transfers between devices, with_halo(): after = lax.ppermute(leading, axis, down)  11.3 us
  transfers between devices with their start and end apart: 15, of which 10 were waited for; matrix products, arithmetic and copies ran while one was open for 0% of the time, Pallas kernels for 0%

profile of v1, /device:TPU:2, one launch (start us, length us, event | category | flops | bytes accessed | tf_op | source)
XLA Modules:
  0.0 546.5 jit_solution(3365145714008128622)
XLA Ops:
  7.5 1.6 stack.6
  9.1 12.8 %all-to-all-start = ((bf16[16,64,1024]{2,1,0:T(8,128)(2,1)}), bf16[16,64,1024]{2,1,0:T(8,128)(2,1)S(1)}, u32[]{:S(2)}, u32[]{:S(2)}) async-start(bf16[16,64,1024]{2,1,0:T(8,128)(2,1)} %stack.6), calls=%async_computation | async-start | bytes 4194304 | tf_op jit(solution)/shard_map/all_to_all | solution.py:54
  22.0 8.2 %collective-permute-start = (f32[8,1,128]{2,0,1:T(8,128)S(1)}, f32[8,1,128]{2,0,1:T(8,128)S(1)}, u32[]{:S(2)}, u32[]{:S(2)}) collective-permute-start(f32[8,1,128]{2,0,1:T(8,128)S(1)} %copy.34), channel_id=1, source_target_pairs={{0,4},{4,8},{8,12},{12,16},{16,20},{20,24},{24,28},{1,5},{5,9},{9,... | collective-permute-start | bytes 12296 | tf_op jit(solution)/shard_map/ppermute | solution.py:16
  30.2 1.3 collective-permute-start.1
  31.5 31.3 %collective-permute-done = f32[8,1,128]{2,0,1:T(8,128)S(1)} collective-permute-done((f32[8,1,128]{2,0,1:T(8,128)S(1)}, f32[8,1,128]{2,0,1:T(8,128)S(1)}, u32[]{:S(2)}, u32[]{:S(2)}) %collective-permute-start) | collective-permute-done | bytes 4128 | tf_op jit(solution)/shard_map/ppermute | solution.py:16
  62.8 7.1 %collective-permute-done.1 = f32[8,1,128]{2,0,1:T(8,128)S(1)} collective-permute-done((f32[8,1,128]{2,0,1:T(8,128)S(1)}, f32[8,1,128]{2,0,1:T(8,128)S(1)}, u32[]{:S(2)}, u32[]{:S(2)}) %collective-permute-start.1) | collective-permute-done | bytes 4128 | tf_op jit(solution)/shard_map/ppermute | solution.py:17
  69.9 33.0 %all-to-all-done = bf16[16,64,1024]{2,1,0:T(8,128)(2,1)S(1)} async-done(((bf16[16,64,1024]{2,1,0:T(8,128)(2,1)}), bf16[16,64,1024]{2,1,0:T(8,128)(2,1)S(1)}, u32[]{:S(2)}, u32[]{:S(2)}) %all-to-all-start) | async-done | bytes 2097184 | tf_op jit(solution)/shard_map/all_to_all | solution.py:54
  102.8 1.3 copy-done.1
  104.1 2.9 copy.22
  107.8 8.2 %collective-permute-start.4 = (f32[256,1,128]{0,2,1:T(8,128)S(1)}, f32[256,1,128]{0,2,1:T(8,128)S(1)}, u32[]{:S(2)}, u32[]{:S(2)}) collective-permute-start(f32[256,1,128]{0,2,1:T(8,128)S(1)} %get-tuple-element.11), channel_id=1, source_target_pairs={{0,4},{4,8},{8,12},{12,16},{16,20},{20,24},{24,28},{1,5},{5,9},{9,... | collective-permute-start | bytes 393224 | tf_op jit(solution)/shard_map/ppermute | solution.py:16
  116.1 1.3 collective-permute-start.5
  117.5 3.4 collective-permute-start.2
  120.9 2.4 collective-permute-start.3
  123.3 9.6 %collective-permute-done.5 = f32[256,1,128]{0,2,1:T(8,128)S(1)} collective-permute-done((f32[256,1,128]{0,2,1:T(8,128)S(1)}, f32[256,1,128]{0,2,1:T(8,128)S(1)}, u32[]{:S(2)}, u32[]{:S(2)}) %collective-permute-start.5) | collective-permute-done | bytes 131104 | tf_op jit(solution)/shard_map/ppermute | solution.py:17
  132.9 3.4 collective-permute-start.6
  136.3 2.4 collective-permute-start.7
  138.8 1.5 fusion
  140.3 1.5 collective-permute-done.7
  141.9 1.3 fusion.4
  143.2 2.0 convert_bitcast_fusion.1
  145.2 3.9 copy.25
  149.2 128.5 %reduce-scatter.7.cloned.1.call-done = bf16[64,1024]{1,0:T(8,128)(2,1)} async-done(((bf16[1024,1024]{1,0:T(8,128)(2,1)}), bf16[64,1024]{1,0:T(8,128)(2,1)}) %reduce-scatter.7.cloned.1.call-update) | async-done | bytes 131088
  279.4 96.9 %all_to_all.10 = bf16[16,64,1024]{2,1,0:T(8,128)(2,1)S(1)} all-to-all(bf16[16,64,1024]{2,1,0:T(8,128)(2,1)S(1)} %stack.7), channel_id=1, replica_groups=mesh['quad'=16,'gy'=8,'gx'=4] {'quad'}, dimensions={0} | all-to-all | bytes 4194304 | tf_op jit(solution)/shard_map/all_to_all | solution.py:54
  377.0 11.8 %collective-permute-start.8 = (f32[256,1,128]{0,2,1:T(8,128)S(1)}, f32[256,1,128]{0,2,1:T(8,128)S(1)}, u32[]{:S(2)}, u32[]{:S(2)}) collective-permute-start(f32[256,1,128]{0,2,1:T(8,128)S(1)} %get-tuple-element.9), channel_id=1, source_target_pairs={{0,4},{4,8},{8,12},{12,16},{16,20},{20,24},{24,28},{1,5},{5,9},{9,... | collective-permute-start | bytes 393224 | tf_op jit(solution)/shard_map/ppermute | solution.py:16
  390.1 4.8 collective-permute-done.8
  394.8 11.2 %collective-permute-done.9 = f32[256,1,128]{0,2,1:T(8,128)S(1)} collective-permute-done((f32[256,1,128]{0,2,1:T(8,128)S(1)}, f32[256,1,128]{0,2,1:T(8,128)S(1)}, u32[]{:S(2)}, u32[]{:S(2)}) %collective-permute-start.9) | collective-permute-done | bytes 131104 | tf_op jit(solution)/shard_map/ppermute | solution.py:17
  406.1 3.3 collective-permute-start.10
  409.4 2.5 collective-permute-start.11
  411.9 3.0 collective-permute-done.11
  414.9 1.3 fusion.8
  417.0 2.6 copy.27
  419.6 118.0 %reduce-scatter.9.cloned.1.call-done = bf16[64,1024]{1,0:T(8,128)(2,1)} async-done(((bf16[1024,1024]{1,0:T(8,128)(2,1)}), bf16[64,1024]{1,0:T(8,128)(2,1)}) %reduce-scatter.9.cloned.1.call-update) | async-done | bytes 131088
  (48 shorter events, 8.5 us)
Async XLA Ops:
  6.5 100.5 %copy-start = (bf16[256,1024]{1,0:T(8,128)(2,1)S(1)}, bf16[256,1024]{1,0:T(8,128)(2,1)}, u32[]{:S(2)}) copy-start(bf16[256,1024]{1,0:T(8,128)(2,1)} %param.7) | copy-start | bytes 1572868
  9.1 12.8 %copy-start.3 = (f32[8,8,128]{2,1,0:T(8,128)S(1)}, f32[8,8,128]{2,1,0:T(8,128)}, u32[]{:S(2)}) copy-start(f32[8,8,128]{2,1,0:T(8,128)} %param.10) | copy-start | bytes 98308
  9.1 93.7 %all-to-all-start = ((bf16[16,64,1024]{2,1,0:T(8,128)(2,1)}), bf16[16,64,1024]{2,1,0:T(8,128)(2,1)S(1)}, u32[]{:S(2)}, u32[]{:S(2)}) async-start(bf16[16,64,1024]{2,1,0:T(8,128)(2,1)} %stack.6), calls=%async_computation | async-start | bytes 4194304 | tf_op jit(solution)/shard_map/all_to_all | solution.py:54
  21.9 255.8 %reduce-scatter.7.cloned.1.call-start = ((), (), s32[]{:S(2)}) async-start(), calls=%async_computation.4 | async-start | bytes 2228224
  22.0 40.8 %collective-permute-start = (f32[8,1,128]{2,0,1:T(8,128)S(1)}, f32[8,1,128]{2,0,1:T(8,128)S(1)}, u32[]{:S(2)}, u32[]{:S(2)}) collective-permute-start(f32[8,1,128]{2,0,1:T(8,128)S(1)} %copy.34), channel_id=1, source_target_pairs={{0,4},{4,8},{8,12},{12,16},{16,20},{20,24},{24,28},{1,5},{5,9},{9,... | collective-permute-start | bytes 12296 | tf_op jit(solution)/shard_map/ppermute | solution.py:16
  30.2 39.7 %collective-permute-start.1 = (f32[8,1,128]{2,0,1:T(8,128)S(1)}, f32[8,1,128]{2,0,1:T(8,128)S(1)}, u32[]{:S(2)}, u32[]{:S(2)}) collective-permute-start(f32[8,1,128]{2,0,1:T(8,128)S(1)} %copy.35), channel_id=1, source_target_pairs={{4,0},{8,4},{12,8},{16,12},{20,16},{24,20},{28,24},{5,1},{9,5},{13... | collective-permute-start | bytes 12296 | tf_op jit(solution)/shard_map/ppermute | solution.py:17
  102.8 1.3 copy-start.1
  107.0 31.8 %copy-start.4 = (f32[256,8]{0,1:T(8,128)S(1)}, f32[256,8]{0,1:T(8,128)}, u32[]{:S(2)}) copy-start(f32[256,8]{0,1:T(8,128)} %param.9) | copy-start | bytes 24580
  107.8 34.1 %copy-start.5 = (f32[256]{0:T(256)S(1)}, f32[256]{0:T(256)}, u32[]{:S(2)}) copy-start(f32[256]{0:T(256)} %param.11) | copy-start | bytes 3076
  107.8 34.1 %copy-start.6 = (f32[256]{0:T(256)S(1)}, f32[256]{0:T(256)}, u32[]{:S(2)}) copy-start(f32[256]{0:T(256)} %param.8) | copy-start | bytes 3076
  107.8 15.5 %collective-permute-start.4 = (f32[256,1,128]{0,2,1:T(8,128)S(1)}, f32[256,1,128]{0,2,1:T(8,128)S(1)}, u32[]{:S(2)}, u32[]{:S(2)}) collective-permute-start(f32[256,1,128]{0,2,1:T(8,128)S(1)} %get-tuple-element.11), channel_id=1, source_target_pairs={{0,4},{4,8},{8,12},{12,16},{16,20},{20,24},{24,28},{1,5},{5,9},{9,... | collective-permute-start | bytes 393224 | tf_op jit(solution)/shard_map/ppermute | solution.py:16
  116.1 16.8 %collective-permute-start.5 = (f32[256,1,128]{0,2,1:T(8,128)S(1)}, f32[256,1,128]{0,2,1:T(8,128)S(1)}, u32[]{:S(2)}, u32[]{:S(2)}) collective-permute-start(f32[256,1,128]{0,2,1:T(8,128)S(1)} %get-tuple-element.12), channel_id=1, source_target_pairs={{4,0},{8,4},{12,8},{16,12},{20,16},{24,20},{28,24},{5,1},{9,5},{13... | collective-permute-start | bytes 393224 | tf_op jit(solution)/shard_map/ppermute | solution.py:17
  117.5 21.3 %collective-permute-start.2 = (f32[8,10,1]{2,0,1:T(8,128)S(1)}, f32[8,10,1]{2,0,1:T(8,128)S(1)}, u32[]{:S(2)}, u32[]{:S(2)}) collective-permute-start(f32[8,10,1]{2,0,1:T(8,128)S(1)} %get-tuple-element.13), channel_id=1, source_target_pairs={{0,1},{1,2},{2,3},{4,5},{5,6},{6,7},{8,9},{9,10},{10,11},{12,13},{... | collective-permute-start | bytes 968 | tf_op jit(solution)/shard_map/ppermute | solution.py:16
  120.9 17.9 %collective-permute-start.3 = (f32[8,10,1]{2,0,1:T(8,128)S(1)}, f32[8,10,1]{2,0,1:T(8,128)S(1)}, u32[]{:S(2)}, u32[]{:S(2)}) collective-permute-start(f32[8,10,1]{2,0,1:T(8,128)S(1)} %get-tuple-element.14), channel_id=1, source_target_pairs={{1,0},{2,1},{3,2},{5,4},{6,5},{7,6},{9,8},{10,9},{11,10},{13,12},{... | collective-permute-start | bytes 968 | tf_op jit(solution)/shard_map/ppermute | solution.py:17
  132.9 7.4 %collective-permute-start.6 = (f32[256,10,1]{0,2,1:T(1,128)S(1)}, f32[256,10,1]{0,2,1:T(1,128)S(1)}, u32[]{:S(2)}, u32[]{:S(2)}) collective-permute-start(f32[256,10,1]{0,2,1:T(1,128)S(1)} %get-tuple-element.7), channel_id=1, source_target_pairs={{0,1},{1,2},{2,3},{4,5},{5,6},{6,7},{8,9},{9,10},{10,11},{12,13},{... | collective-permute-start | bytes 30728 | tf_op jit(solution)/shard_map/ppermute | solution.py:16
  136.3 5.6 %collective-permute-start.7 = (f32[256,10,1]{0,2,1:T(1,128)S(1)}, f32[256,10,1]{0,2,1:T(1,128)S(1)}, u32[]{:S(2)}, u32[]{:S(2)}) collective-permute-start(f32[256,10,1]{0,2,1:T(1,128)S(1)} %get-tuple-element.8), channel_id=1, source_target_pairs={{1,0},{2,1},{3,2},{5,4},{6,5},{7,6},{9,8},{10,9},{11,10},{13,12},{... | collective-permute-start | bytes 30728 | tf_op jit(solution)/shard_map/ppermute | solution.py:17
  149.1 129.9 %copy-start.2 = (bf16[64,8,128]{2,1,0:T(8,128)(2,1)S(1)}, bf16[64,8,128]{2,1,0:T(8,128)(2,1)}, u32[]{:S(2)}) copy-start(bf16[64,8,128]{2,1,0:T(8,128)(2,1)} %param.6) | copy-start | bytes 393220
  149.2 388.4 %reduce-scatter.9.cloned.1.call-start = ((), (), s32[]{:S(2)}) async-start(), calls=%async_computation.5 | async-start | bytes 2228224
  377.0 17.8 %collective-permute-start.8 = (f32[256,1,128]{0,2,1:T(8,128)S(1)}, f32[256,1,128]{0,2,1:T(8,128)S(1)}, u32[]{:S(2)}, u32[]{:S(2)}) collective-permute-start(f32[256,1,128]{0,2,1:T(8,128)S(1)} %get-tuple-element.9), channel_id=1, source_target_pairs={{0,4},{4,8},{8,12},{12,16},{16,20},{20,24},{24,28},{1,5},{5,9},{9,... | collective-permute-start | bytes 393224 | tf_op jit(solution)/shard_map/ppermute | solution.py:16
  388.8 17.2 %collective-permute-start.9 = (f32[256,1,128]{0,2,1:T(8,128)S(1)}, f32[256,1,128]{0,2,1:T(8,128)S(1)}, u32[]{:S(2)}, u32[]{:S(2)}) collective-permute-start(f32[256,1,128]{0,2,1:T(8,128)S(1)} %get-tuple-element.10), channel_id=1, source_target_pairs={{4,0},{8,4},{12,8},{16,12},{20,16},{24,20},{28,24},{5,1},{9,5},{13... | collective-permute-start | bytes 393224 | tf_op jit(solution)/shard_map/ppermute | solution.py:17
  406.1 5.9 %collective-permute-start.10 = (f32[256,10,1]{0,2,1:T(1,128)S(1)}, f32[256,10,1]{0,2,1:T(1,128)S(1)}, u32[]{:S(2)}, u32[]{:S(2)}) collective-permute-start(f32[256,10,1]{0,2,1:T(1,128)S(1)} %get-tuple-element.5), channel_id=1, source_target_pairs={{0,1},{1,2},{2,3},{4,5},{5,6},{6,7},{8,9},{9,10},{10,11},{12,13},{... | collective-permute-start | bytes 30728 | tf_op jit(solution)/shard_map/ppermute | solution.py:16
  409.4 5.6 %collective-permute-start.11 = (f32[256,10,1]{0,2,1:T(1,128)S(1)}, f32[256,10,1]{0,2,1:T(1,128)S(1)}, u32[]{:S(2)}, u32[]{:S(2)}) collective-permute-start(f32[256,10,1]{0,2,1:T(1,128)S(1)} %get-tuple-element.6), channel_id=1, source_target_pairs={{1,0},{2,1},{3,2},{5,4},{6,5},{7,6},{9,8},{10,9},{11,10},{13,12},{... | collective-permute-start | bytes 30728 | tf_op jit(solution)/shard_map/ppermute | solution.py:17
Sparse Core Ops, SparseCore 0:
  149.3 128.3 reduce-scatter.6
  419.7 117.8 reduce-scatter.8
